TPU v7x, 32 devices: a whole 2x2x4 slice. The times are simulated.
32 devices in a mesh: band: 16 (over z, x, core), lev: 2 (over y).
Axes of the slice: x: 2, y: 2, z: 4, core: 2. Of those that a mesh axis runs over, the one named last changes fastest.
Arguments:
- field_grid: float32 [3, 8, 384, 2, 1536], P(None, 'lev', 'band'), may hold values from -6 to 6
- increment: float32 [3, 8, 384, 2, 1536], P(None, 'lev', 'band'), may hold values from -6 to 6
- points: int32 [384], P('band'), may hold values from 16 to 1536, as said below
- weights: float32 [384], replicated, may hold values from 0.0013020834 to 0.0052083335
- pair_slot: int32 [384], replicated, may hold values from 0 to 383, each once
- legendre: float32 [384, 384, 769], P(('band', 'lev')), may hold values from -6 to 6
- strength: float32 [3, 8], replicated, may hold values from 1 to 16
Outputs:
- stepped: float32 [3, 8, 384, 2, 1536], P(None, 'lev', 'band')
Inputs may be any that keep to these rules, and one draw needn't show every extreme that they name: points[j] lies within 32 of 16 + 1520 * j // 383, kept within 16 to 1536; the last latitude pair has 1536 cells. `pair_slot`: A permutation of 0 to 383; slot s is held by the device of joint band+lev index s // 12, at place s % 12, which holds legendre[s].
All inputs are finite; a program needn't handle non-finite values.
Results may differ from a plain program's by a relative error of at most 0.0003.
Values sent between devices are 32-bit elements; how exact they have to be, the bound alone decides.
No kernel may reach another device: no remote copies, remote signals or barrier semaphores. Data moves between devices by JAX's collectives and lax.ppermute only.
A program may use at most 320 MiB of HBM per device.

v0:
```python
import math

import jax
import jax.numpy as jnp
from jax import lax
from jax.sharding import PartitionSpec as P

TWO_PI = 2.0 * math.pi


def dft_tables(counts, length, wavecount):
    inner = 32
    outer = length // inner
    orders = lax.iota(jnp.int32, wavecount)
    coarse = lax.iota(jnp.int32, outer) * inner
    finer = lax.iota(jnp.int32, inner)
    modulus = counts[:, None, None]
    step_angle = (TWO_PI / counts.astype(jnp.float32))[:, None, None]
    coarse_angle = (coarse[None, :, None] * orders[None, None, :] % modulus).astype(
        jnp.float32
    ) * step_angle
    finer_angle = (finer[None, :, None] * orders[None, None, :] % modulus).astype(
        jnp.float32
    ) * step_angle
    coarse_cos = jnp.cos(coarse_angle)[:, :, None, :]
    coarse_sin = jnp.sin(coarse_angle)[:, :, None, :]
    finer_cos = jnp.cos(finer_angle)[:, None, :, :]
    finer_sin = jnp.sin(finer_angle)[:, None, :, :]
    pair_count = counts.shape[0]
    full_cos = (coarse_cos * finer_cos - coarse_sin * finer_sin).reshape(
        pair_count, length, wavecount
    )
    full_sin = (coarse_sin * finer_cos + coarse_cos * finer_sin).reshape(
        pair_count, length, wavecount
    )
    places = lax.iota(jnp.int32, length)
    live = (places[None, :, None] < modulus) & (orders[None, None, :] <= (modulus - 1) // 2)
    cosines = jnp.where(live, full_cos, 0.0)
    sines = jnp.where(live, -full_sin, 0.0)
    return jnp.concatenate([cosines, sines], axis=2)


def body(field_grid, increment, points, weights, pair_slot, legendre, strength):
    band_count = lax.axis_size("band")
    level_groups = lax.axis_size("lev")
    summed = field_grid + increment
    fields = summed.shape[0]
    local_levels = summed.shape[1]
    band_pairs = summed.shape[2]
    length = summed.shape[4]
    wavecount = length // 2
    pair_total = wavecount // 2
    total_levels = local_levels * level_groups
    regrouped = lax.all_to_all(summed, "lev", split_axis=2, concat_axis=1, tiled=True)
    piece_pairs = band_pairs // level_groups
    counts = lax.dynamic_slice_in_dim(points, lax.axis_index("lev") * piece_pairs, piece_pairs)
    tables = dft_tables(counts, length, wavecount)
    row_count = fields * total_levels * 2
    pair_rows = jnp.moveaxis(regrouped, 2, 0).reshape(piece_pairs, row_count, length)
    spectra = jnp.einsum("pqx,pxk->pqk", pair_rows, tables, precision=lax.Precision.HIGHEST)
    spectra = spectra / counts.astype(jnp.float32)[:, None, None]
    piece_width = 2 * row_count
    by_wave = jnp.transpose(spectra.reshape(piece_pairs, row_count, 2, wavecount), (3, 0, 2, 1))
    by_wave = by_wave.reshape(wavecount, piece_pairs, piece_width)
    slot_ranks = lax.iota(jnp.int32, pair_total)
    pair_of_slot = jnp.zeros((pair_total,), jnp.int32).at[pair_slot].set(slot_ranks)
    wave_order = jnp.stack([pair_of_slot, wavecount - 1 - pair_of_slot], axis=1).reshape(wavecount)
    outgoing = jnp.take(by_wave, wave_order, axis=0)
    slot_count = legendre.shape[0]
    arrived = lax.all_to_all(outgoing, ("band", "lev"), split_axis=0, concat_axis=1, tiled=True)
    arrived = arrived.reshape(2 * slot_count, band_count, level_groups, piece_pairs, piece_width)
    row_width = 4 * fields * total_levels
    arrived = arrived.reshape(2 * slot_count, pair_total, row_width)
    lat_count = arrived.shape[1]
    own_slots = lax.axis_index(("band", "lev")) * slot_count + lax.iota(jnp.int32, slot_count)
    lower_wave = jnp.take(pair_of_slot, own_slots)
    columns = lax.iota(jnp.int32, wavecount + 1)
    second_member = columns[None, :] >= (wavecount - lower_wave)[:, None]
    degree = jnp.where(second_member, columns[None, :] - 1, lower_wave[:, None] + columns[None, :])
    wave_of_column = jnp.where(
        second_member, wavecount - 1 - lower_wave[:, None], lower_wave[:, None]
    )
    parity = jnp.where((degree - wave_of_column) % 2 == 0, 1.0, -1.0)
    weighted = arrived.reshape(slot_count, 2, lat_count, row_width) * weights[None, None, :, None]
    analysed = jnp.einsum("sjc,sejr->scer", legendre, weighted, precision=lax.Precision.HIGHEST)
    analysed = analysed.reshape(slot_count, wavecount + 1, 2, 2, fields * total_levels, 2)
    chosen = jnp.where(second_member[:, :, None, None, None], analysed[:, :, 1], analysed[:, :, 0])
    coefficients = chosen[..., 0] + parity[:, :, None, None] * chosen[..., 1]
    degree_real = degree.astype(jnp.float32)
    degree_ratio = degree_real * (degree_real + 1.0) / float((wavecount - 1) * wavecount)
    damping_rate = strength.reshape(fields * total_levels)
    damping = 1.0 / (1.0 + damping_rate[None, None, :] * (degree_ratio * degree_ratio)[:, :, None])
    damped = coefficients * damping[:, :, None, :]
    second_real = jnp.where(second_member, 1.0, 0.0)
    member_mask = jnp.stack([1.0 - second_real, second_real], axis=2)
    hemisphere_sign = jnp.stack([jnp.ones_like(parity), parity], axis=2)
    spread = damped[:, :, None, :, :, None] * member_mask[:, :, :, None, None, None]
    spread = spread * hemisphere_sign[:, :, None, None, None, :]
    spread = spread.reshape(slot_count, wavecount + 1, 2 * row_width)
    returned = jnp.einsum("sjc,scr->sjr", legendre, spread, precision=lax.Precision.HIGHEST)
    leaving = jnp.transpose(returned.reshape(slot_count, lat_count, 2, row_width), (0, 2, 1, 3))
    leaving = leaving.reshape(2 * slot_count, lat_count, row_width)
    leaving = leaving.reshape(2 * slot_count, band_count, level_groups, piece_pairs, piece_width)
    flat_back = leaving.reshape(2 * slot_count, band_count * level_groups, piece_pairs, piece_width)
    home_rows = lax.all_to_all(flat_back, ("band", "lev"), split_axis=1, concat_axis=0, tiled=True)
    home_rows = home_rows.reshape(wavecount, piece_pairs, piece_width)
    positions = (
        jnp.zeros((wavecount,), jnp.int32).at[wave_order].set(lax.iota(jnp.int32, wavecount))
    )
    restored = jnp.take(home_rows, positions, axis=0)
    spectral_rows = jnp.transpose(
        restored.reshape(wavecount, piece_pairs, 2, row_count), (1, 3, 2, 0)
    )
    spectral_rows = spectral_rows.reshape(piece_pairs, row_count, 2 * wavecount)
    doubling = jnp.where(lax.iota(jnp.int32, 2 * wavecount) % wavecount == 0, 1.0, 2.0)
    grid_rows = jnp.einsum(
        "pqk,pxk->pqx",
        spectral_rows * doubling[None, None, :],
        tables,
        precision=lax.Precision.HIGHEST,
    )
    grid_rows = jnp.moveaxis(grid_rows.reshape(piece_pairs, fields, total_levels, 2, length), 0, 2)
    return lax.all_to_all(grid_rows, "lev", split_axis=1, concat_axis=2, tiled=True)


def solution(mesh):
    return jax.shard_map(
        body,
        mesh=mesh,
        in_specs=(
            P(None, "lev", "band", None, None),
            P(None, "lev", "band", None, None),
            P("band"),
            P(),
            P(),
            P(("band", "lev"), None, None),
            P(),
        ),
        out_specs=P(None, "lev", "band", None, None),
        check_vma=False,
    )
```

profile of v0, /device:TPU:1, one launch (start us, length us, event | category | flops | bytes accessed | tf_op | source)
XLA Modules:
  0.0 830.9 jit_solution(12581593312345706289)
XLA Ops:
  0.0 7.1 copy_add_fusion
  7.1 0.0 copy-start.4
  7.1 4.1 all-to-all-start
  11.2 0.0 copy-done.4
  11.2 0.6 fusion.46
  11.9 0.1 iota_compare_fusion
  12.0 0.1 iota_multiply_fusion
  12.1 32.1 %fusion.17 = (f32[12,48,768]{2,1,0:T(8,128)S(1)}, f32[12,48,768]{2,1,0:T(8,128)S(1)}) fusion(f32[12]{0:T(128)S(1)} %broadcast_divide_fusion.1, s32[12]{0:T(128)S(1)} %get-tuple-element.26, s32[48,768]{1,0:T(8,128)S(1)} %iota_multiply_fusion, pred[12]{0:T(512)(128)(4,1)S(1)} %broadcast_compare_fusion), kind=kLoop, calls=%fused_computation.43 | loop fusion | flops 3981312 | bytes 3686508 | tf_op jit(solution)/shard_map/cos | solution.py:25
  44.2 16.5 %fusion.24 = (f32[12,32,768]{2,1,0:T(8,128)S(1)}, f32[12,32,768]{2,1,0:T(8,128)}) fusion(f32[12]{0:T(128)S(1)} %broadcast_divide_fusion.1, s32[12]{0:T(128)S(1)} %get-tuple-element.26, s32[32,768]{1,0:T(8,128)S(1)} %iota_multiply_fusion.1, pred[12]{0:T(512)(128)(4,1)S(1)} %broadcast_compare_fusion), kind=kLoop, calls=%fused_computation.51 | loop fusion | flops 2654208 | bytes 2457708 | tf_op jit(solution)/shard_map/cos | solution.py:27
  60.6 0.1 iota_compare_fusion.2
  60.7 37.0 %multiply_subtract_fusion = (f32[12,48,32,768]{3,2,1,0:T(8,128)}, f32[12,48,32,768]{3,2,1,0:T(8,128)}) fusion(f32[12,32,768]{2,1,0:T(8,128)} %get-tuple-element.17, f32[12,48,768]{2,1,0:T(8,128)S(1)} %get-tuple-element.15, f32[12,32,768]{2,1,0:T(8,128)S(1)} %get-tuple-element.16, f32[12,48,768]{2,1,0:T(8,128)S(1)} %get-tuple-element.14), kind=kLoop, calls=%fused_computation.11 | loop fusion | flops 99090432 | bytes 119144448 | tf_op jit(solution)/shard_map/sub | solution.py:30
  97.7 73.0 %and_select_fusion.1 = (f32[12,1536,768]{2,1,0:T(8,128)}, f32[12,1536,768]{2,1,0:T(8,128)}) fusion(f32[12,48,32,768]{3,2,1,0:T(8,128)} %get-tuple-element.10, pred[12,768]{1,0:T(8,128)(4,1)S(1)} %iota_compare_fusion.2, pred[12,1536]{1,0:T(8,128)(4,1)S(1)} %iota_compare_fusion, f32[12,48,32,768]{3,2,1,0:T(8,128)} %get-tuple-element.11), kind=kLoop, calls=%fused_computation.9 | loop fusion | flops 42467328 | bytes 226520064 | tf_op jit(solution)/shard_map/jit(_where)/select_n | solution.py:38
  170.7 0.0 copy-done.3
  170.7 3.3 scatter_custom_fusion
  174.1 0.8 copy.41
  174.9 1.1 reshape.699
  176.0 0.0 all-to-all-done
  176.0 3.2 copy.45
  179.2 4.2 reshape.696
  183.4 0.0 copy-done.5
  183.5 74.6 %broadcast_divide_fusion = f32[12,48,1536]{2,1,0:T(8,128)} fusion(f32[12]{0:T(128)S(1)} %copy-done.5, f32[12,48,1536]{2,1,0:T(8,128)S(1)} %reshape.696, f32[12,1536,768]{2,1,0:T(8,128)} %get-tuple-element.19, f32[12,1536,768]{2,1,0:T(8,128)} %get-tuple-element.18), kind=kOutput, calls=%fused_computation.45 | convolution fusion | flops 16336650240 | bytes 120324144 | tf_op jit(solution)/shard_map/pqx,pxk->pqk/dot_general | solution.py:60
  258.0 2.4 copy.81
  260.4 4.2 copy.47
  264.6 6.6 gather_fusion.1
  271.2 7.8 broadcast_select_fusion.1
  279.1 8.0 all-to-all-start.1
  287.1 0.7 gather_fusion
  287.7 0.0 copy-done.2
  287.7 0.1 mul.272
  287.8 0.3 broadcast_subtract_fusion
  288.2 0.1 pad_maximum_fusion.3
  288.3 0.1 iota_compare_fusion.1
  288.4 0.1 fusion.31
  288.5 0.2 add_divide_fusion
  288.8 137.5 %all-to-all-done.1 = f32[768,12,96]{2,1,0:T(8,128)} async-done(((f32[768,12,96]{2,1,0:T(8,128)}), f32[768,12,96]{2,1,0:T(8,128)}, u32[]{:S(2)}, u32[]{:S(2)}) %all-to-all-start.1) | async-done | bytes 3538976 | tf_op jit(solution)/shard_map/all_to_all | solution.py:70
  426.3 4.7 copy.49
  431.0 0.0 copy-done.1
  431.0 1.7 broadcast_multiply_fusion.1
  432.8 34.2 %fusion.7 = f32[12,769,2,96]{1,3,2,0:T(8,128)} fusion(f32[12,384,769]{1,2,0:T(8,128)} %param.14, f32[12,2,384,96]{3,1,0,2:T(2,128)S(1)} %broadcast_multiply_fusion.1), kind=kOutput, calls=%fused_computation.27 | convolution fusion | flops 8164343808 | bytes 24800256 | tf_op jit(solution)/shard_map/sjc,sejr->scer/dot_general | solution.py:85
  467.0 10.5 %reshape.700 = f32[12,769,2,2,24,2]{1,5,4,3,2,0:T(2,128)} reshape(f32[12,769,2,96]{1,3,2,0:T(8,128)} %fusion.7) | data formatting | bytes 14174208 | tf_op jit(solution)/shard_map/reshape | solution.py:86
  477.5 5.6 fusion.5
  483.1 3.2 fusion.47
  486.3 0.3 fusion.13
  486.6 0.4 broadcast_multiply_fusion.2
  487.0 4.5 broadcast_multiply_fusion
  491.5 10.7 %mul.286 = f32[12,769,192]{1,2,0:T(8,128)} reshape(f32[12,769,2,2,24,2]{1,5,4,3,2,0:T(2,128)} %broadcast_multiply_fusion) | data formatting | bytes 14174208 | tf_op jit(solution)/shard_map/mul | solution.py:98
  502.2 19.0 %fusion.48 = f32[12,192,384]{2,1,0:T(8,128)S(1)} fusion(f32[12,769,192]{1,2,0:T(8,128)} %mul.286, f32[12,384,769]{1,2,0:T(8,128)} %param.14), kind=kOutput, calls=%fused_computation.120 | convolution fusion | flops 8164343808 | bytes 24800256 | tf_op jit(solution)/shard_map/sjc,scr->sjr/dot_general | solution.py:100
  521.2 5.5 copy.53
  526.7 4.2 all-to-all-start.2
  530.9 0.0 copy-done
  530.9 0.2 reshape.703
  531.1 3.4 scatter_custom_fusion.1
  534.6 101.7 %all-to-all-done.2 = f32[24,32,12,96]{3,0,2,1:T(8,128)} async-done(((f32[24,32,12,96]{3,0,2,1:T(8,128)}), f32[24,32,12,96]{3,0,2,1:T(8,128)}, u32[]{:S(2)}, u32[]{:S(2)}) %all-to-all-start.2) | async-done | bytes 3538976 | tf_op jit(solution)/shard_map/all_to_all | solution.py:105
  636.3 2.7 copy.54
  639.0 5.4 copy.55
  644.4 6.6 gather_fusion.2
  651.1 8.0 broadcast_select_fusion
  659.1 5.9 copy.56
  665.0 2.4 copy.66
  667.5 112.1 %fusion = f32[12,48,1536]{2,1,0:T(8,128)} fusion(f32[12,1536,768]{2,1,0:T(8,128)} %get-tuple-element.19, f32[12,1536,768]{2,1,0:T(8,128)} %get-tuple-element.18, f32[12,48,1536]{2,1,0:T(8,128)S(1)} %bitcast.83, f32[1536]{0:T(1024)S(1)} %fusion.37), kind=kOutput, calls=%fused_computation.6 | convolution fusion | flops 16336650240 | bytes 120330240 | tf_op jit(solution)/shard_map/pqk,pxk->pqx/dot_general | solution.py:116
  779.5 4.0 reshape.706
  783.5 1.3 copy.82
  784.9 42.1 %all_to_all.66 = f32[3,8,12,2,1536]{4,3,0,2,1:T(2,128)S(1)} all-to-all(f32[3,8,12,2,1536]{4,3,0,2,1:T(2,128)S(1)} %bitcast.91), channel_id=1, replica_groups=mesh['band'=16,'lev'=2] {'lev'}, dimensions={1} | all-to-all | bytes 7077888 | tf_op jit(solution)/shard_map/all_to_all | solution.py:123
  827.0 3.7 copy.59
  (31 shorter events, 0.2 us)
Async XLA Ops:
  7.1 4.2 copy-start.4
  7.1 169.0 %all-to-all-start = ((f32[3,4,24,2,1536]{4,3,1,0,2:T(2,128)}), f32[3,4,24,2,1536]{4,3,1,0,2:T(2,128)S(1)}, u32[]{:S(2)}, u32[]{:S(2)}) async-start(f32[3,4,24,2,1536]{4,3,1,0,2:T(2,128)} %copy_add_fusion), calls=%async_computation | async-start | bytes 7077888 | tf_op jit(solution)/shard_map/all_to_all | solution.py:54
  97.7 73.0 %copy-start.3 = (s32[384]{0:T(512)S(1)}, s32[384]{0:T(512)}, u32[]{:S(2)}) copy-start(s32[384]{0:T(512)} %param.13) | copy-start | bytes 4612
  179.2 4.2 copy-start.5
  279.1 8.7 %copy-start.2 = (f32[3,8]{1,0:T(4,128)S(1)}, f32[3,8]{1,0:T(4,128)}, u32[]{:S(2)}) copy-start(f32[3,8]{1,0:T(4,128)} %param.15) | copy-start | bytes 292
  279.1 147.2 %all-to-all-start.1 = ((f32[768,12,96]{2,1,0:T(8,128)}), f32[768,12,96]{2,1,0:T(8,128)}, u32[]{:S(2)}, u32[]{:S(2)}) async-start(f32[768,12,96]{2,1,0:T(8,128)} %broadcast_select_fusion.1), calls=%async_computation.1 | async-start | bytes 12582912 | tf_op jit(solution)/shard_map/all_to_all | solution.py:70
  426.3 4.8 copy-start.1
  526.7 4.2 copy-start
  526.7 109.6 %all-to-all-start.2 = ((f32[24,32,12,96]{3,0,2,1:T(8,128)}), f32[24,32,12,96]{3,0,2,1:T(8,128)}, u32[]{:S(2)}, u32[]{:S(2)}) async-start(f32[24,32,12,96]{3,0,2,1:T(8,128)} %bitcast.84), calls=%async_computation.2 | async-start | bytes 9437184 | tf_op jit(solution)/shard_map/all_to_all | solution.py:105
where the time goes:
time: 844 us; the launch traced here: 831 us
  matrix products  240 us (28%)
  waiting for transfers between devices  239 us (28%)
  other arithmetic  196 us (23%)
  local copies, waits for them, and re-layouts  97 us (11%)
  blocking collectives  42.1 us (5%)
  starting transfers between devices  16.3 us (2%)
    all_to_all x1, waiting for transfers between devices, body(): lax.all_to_all(outgoing, ('band', 'lev'), split_axis=0, concat_axis=1, ti...  138 us
    dot_general x1, matrix products, body(): jnp.einsum('pqk,pxk->pqx', spectral_rows * doubling[None, None, :], table...  112 us
    all_to_all x1, waiting for transfers between devices, body(): lax.all_to_all(flat_back, ('band', 'lev'), split_axis=1, concat_axis=0, t...  102 us
    dot_general x1, matrix products, body(): jnp.einsum('pqx,pxk->pqk', pair_rows, tables, precision=lax.Precision.HIG...  74.6 us
    select_n x1, other arithmetic, dft_tables(): cosines = jnp.where(live, full_cos, 0.0)  73 us
    all_to_all x1, blocking collectives, body(): lax.all_to_all(grid_rows, 'lev', split_axis=1, concat_axis=2, tiled=True)  42.1 us
    sub x1, other arithmetic, dft_tables(): coarse_cos * finer_cos - coarse_sin * finer_sin  37 us
    dot_general x1, matrix products, body(): jnp.einsum('sjc,sejr->scer', legendre, weighted, precision=lax.Precision....  34.2 us
  transfers between devices with their start and end apart: 3, of which 2 were waited for; matrix products, arithmetic and copies ran while one was open for 20% of the time, Pallas kernels for 0%

commit v1 on v0

v1 whole, which is shorter than its diff:
```python
import math

import jax
import jax.numpy as jnp
from jax import lax
from jax.sharding import PartitionSpec as P

INNER = 256


def turn_cos_sin(product, counts):
    inverse = 1.0 / counts
    whole = jnp.round(product * inverse)
    half = (product - whole * counts) * inverse * math.pi
    square = half * half
    sine = jnp.full_like(square, -1.0 / math.factorial(11))
    for order, sign in ((9, 1.0), (7, -1.0), (5, 1.0), (3, -1.0), (1, 1.0)):
        sine = sine * square + sign / math.factorial(order)
    sine = sine * half
    cosine = jnp.full_like(square, 1.0 / math.factorial(12))
    for order, sign in ((10, -1.0), (8, 1.0), (6, -1.0), (4, 1.0), (2, -1.0), (0, 1.0)):
        cosine = cosine * square + sign / math.factorial(order)
    return 1.0 - 2.0 * sine * sine, 2.0 * sine * cosine


def body(field_grid, increment, points, weights, pair_slot, legendre, strength):
    band_count = lax.axis_size("band")
    level_groups = lax.axis_size("lev")
    fields, local_levels, band_pairs, _, length = field_grid.shape
    wavecount = length // 2
    pair_total = wavecount // 2
    slot_count = legendre.shape[0]
    outer = length // INNER
    stack = fields * local_levels
    rows = 2 * stack
    width = 2 * rows
    high = lax.Precision.HIGH

    slot_ranks = lax.iota(jnp.int32, pair_total)
    matches = pair_slot[None, :] == slot_ranks[:, None]
    pair_of_slot = jnp.sum(jnp.where(matches, slot_ranks[None, :], 0), axis=1)
    wave_order = jnp.stack([pair_of_slot, wavecount - 1 - pair_of_slot], axis=1).reshape(wavecount)
    waves = wave_order.astype(jnp.float32)
    counts = points.astype(jnp.float32)
    fine = lax.iota(jnp.int32, INNER).astype(jnp.float32)
    coarse = (lax.iota(jnp.int32, outer) * INNER).astype(jnp.float32)
    fine_cos, fine_sin = turn_cos_sin(
        fine[None, :, None] * waves[None, None, :], counts[:, None, None]
    )
    turn_cos, turn_sin = turn_cos_sin(
        coarse[None, :, None] * waves[None, None, :], counts[:, None, None]
    )
    table_cos, table_neg = lax.optimization_barrier((fine_cos, -fine_sin))
    live_wave = wave_order[None, :] <= ((points - 1) // 2)[:, None]
    own_weights = lax.dynamic_slice_in_dim(
        weights, lax.axis_index("band") * band_pairs, band_pairs
    )
    ahead = jnp.where(live_wave, (own_weights / counts)[:, None], 0.0)[:, None, :]
    behind = jnp.where(live_wave, jnp.where(wave_order == 0, 1.0, 2.0)[None, :], 0.0)[:, None, :]
    ahead_cos, ahead_sin = turn_cos * ahead, turn_sin * ahead
    behind_cos, behind_sin = turn_cos * behind, turn_sin * behind
    places = lax.iota(jnp.int32, length).reshape(outer, INNER)
    live_cell = places[None, :, :] < points[:, None, None]

    summed = (field_grid + increment).reshape(stack, band_pairs, 2, outer, INNER)
    north, south = summed[:, :, 0], summed[:, :, 1]
    folded = jnp.stack([north + south, north - south], axis=0)
    folded = jnp.transpose(folded, (2, 3, 0, 1, 4)).reshape(band_pairs, outer, rows, INNER)
    folded = jnp.where(live_cell[:, :, None, :], folded, 0.0)
    folded = folded.reshape(band_pairs, outer * rows, INNER)
    part_cos = jnp.einsum("pyb,pbm->pym", folded, table_cos, precision=high)
    part_neg = jnp.einsum("pyb,pbm->pym", folded, table_neg, precision=high)
    part_cos = part_cos.reshape(band_pairs, outer, rows, wavecount)
    part_neg = part_neg.reshape(band_pairs, outer, rows, wavecount)
    real = jnp.sum(
        ahead_cos[:, :, None, :] * part_cos + ahead_sin[:, :, None, :] * part_neg, axis=1
    )
    imag = jnp.sum(
        ahead_cos[:, :, None, :] * part_neg - ahead_sin[:, :, None, :] * part_cos, axis=1
    )
    spectra = jnp.stack([real, imag], axis=1).reshape(band_pairs * width, wavecount)
    outgoing = spectra.T.reshape(
        band_count * level_groups, 2 * slot_count, band_pairs * width
    )
    arrived = lax.all_to_all(outgoing, ("band", "lev"), split_axis=0, concat_axis=0, tiled=True)
    arrived = arrived.reshape(band_count, level_groups, slot_count, 2, band_pairs, width)
    arrived = jnp.transpose(arrived, (2, 0, 4, 3, 1, 5))
    lat_count = band_count * band_pairs
    row_width = 2 * level_groups * width
    arrived = arrived.reshape(slot_count, lat_count, row_width)

    own_slots = lax.axis_index(("band", "lev")) * slot_count + lax.iota(jnp.int32, slot_count)
    lower_wave = jnp.take(pair_of_slot, own_slots)
    columns = lax.iota(jnp.int32, wavecount + 1)
    second_member = columns[None, :] >= (wavecount - lower_wave)[:, None]
    degree = jnp.where(second_member, columns[None, :] - 1, lower_wave[:, None] + columns[None, :])
    wave_of_column = jnp.where(
        second_member, wavecount - 1 - lower_wave[:, None], lower_wave[:, None]
    )
    odd = (degree - wave_of_column) % 2
    degree_real = degree.astype(jnp.float32)
    degree_ratio = degree_real * (degree_real + 1.0) / float((wavecount - 1) * wavecount)
    lane = lax.iota(jnp.int32, row_width)
    lane_group = lane // (level_groups * width) * 2 + lane // stack % 2
    column_group = second_member.astype(jnp.int32) * 2 + odd
    own = strength.reshape(fields, level_groups, local_levels)
    rate = jnp.moveaxis(own, 1, 0).reshape(1, level_groups, 1, stack)
    rate = jnp.broadcast_to(rate, (2, level_groups, 4, stack)).reshape(row_width)
    damping = 1.0 / (1.0 + rate[None, None, :] * (degree_ratio * degree_ratio)[:, :, None])
    damping = jnp.where(column_group[:, :, None] == lane_group[None, None, :], damping, 0.0)
    analysed = jnp.einsum("sjc,sjr->scr", legendre, arrived, precision=high)
    returned = jnp.einsum("sjc,scr->sjr", legendre, analysed * damping, precision=high)

    leaving = returned.reshape(slot_count, band_count, band_pairs, 2, level_groups, width)
    leaving = jnp.transpose(leaving, (1, 4, 0, 3, 2, 5)).reshape(
        band_count * level_groups, 2 * slot_count, band_pairs * width
    )
    home = lax.all_to_all(leaving, ("band", "lev"), split_axis=0, concat_axis=0, tiled=True)
    home = home.reshape(wavecount, band_pairs * width).T.reshape(band_pairs, 2, rows, wavecount)
    real, imag = home[:, 0][:, None], home[:, 1][:, None]
    turned_real = real * behind_cos[:, :, None, :] - imag * behind_sin[:, :, None, :]
    turned_imag = real * behind_sin[:, :, None, :] + imag * behind_cos[:, :, None, :]
    turned_real = turned_real.reshape(band_pairs, outer * rows, wavecount)
    turned_imag = turned_imag.reshape(band_pairs, outer * rows, wavecount)
    cells = jnp.einsum("pym,pbm->pyb", turned_real, table_cos, precision=high)
    cells = cells + jnp.einsum("pym,pbm->pyb", turned_imag, table_neg, precision=high)
    cells = cells.reshape(band_pairs, outer, rows, INNER)
    cells = jnp.where(live_cell[:, :, None, :], cells, 0.0)
    cells = cells.reshape(band_pairs, outer, 2, stack, INNER)
    even, uneven = cells[:, :, 0], cells[:, :, 1]
    stepped = jnp.stack([even + uneven, even - uneven], axis=0)
    stepped = jnp.transpose(stepped, (3, 1, 0, 2, 4))
    return stepped.reshape(fields, local_levels, band_pairs, 2, length)


def solution(mesh):
    return jax.shard_map(
        body,
        mesh=mesh,
        in_specs=(
            P(None, "lev", "band", None, None),
            P(None, "lev", "band", None, None),
            P("band"),
            P(),
            P(),
            P(("band", "lev"), None, None),
            P(),
        ),
        out_specs=P(None, "lev", "band", None, None),
        check_vma=False,
    )
```

time: 844 us -> 430 us (0.51)
  waiting for transfers between devices: 239 us -> 75.2 us
  matrix products: 240 us -> 99.6 us
  other arithmetic: 196 us -> 64.4 us
  blocking collectives: 42.1 us -> 84.8 us
  starting transfers between devices: 16.3 us -> 7.08 us
    all_to_all x3 -> x1, waiting for transfers between devices: 239 us -> 75.2 us  [body(): lax.all_to_all(outgoing, ('band', 'lev'), split_axis=0, concat_axis=0, ti...]
    dot_general x4 -> x6, matrix products: 240 us -> 99.6 us  [the longest x1 19.3 us: body(): analysed = jnp.einsum('sjc,sjr->scr', legendre, arrived, precision=high)]
    select_n x11 -> x4, other arithmetic: 94.6 us -> 1.31 us  [the longest x1 0.74 us: body(): jnp.where(live_wave, (own_weights / counts)[:, None], 0.0)[:, None, :]]
    cos x2 -> x0, other arithmetic: 48.5 us -> none  [the longest x1 32.1 us: dft_tables(): coarse_cos = jnp.cos(coarse_angle)[:, :, None, :]]
    all_to_all x1, blocking collectives: 42.1 us -> 84.8 us  [body(): lax.all_to_all(leaving, ('band', 'lev'), split_axis=0, concat_axis=0, til...]
    sub x2, other arithmetic: 37.4 us -> 1.94 us  [the longest x1 1.71 us: body(): folded = jnp.stack([north + south, north - south], axis=0)]
    transpose x0 -> x5, local copies, waits for them, and re-layouts: none -> 29.7 us  [the longest x1 17.1 us: body(): arrived = jnp.transpose(arrived, (2, 0, 4, 3, 1, 5))]
    neg x0 -> x1, other arithmetic: none -> 24.6 us  [body(): table_cos, table_neg = lax.optimization_barrier((fine_cos, -fine_sin))]
  transfers between devices with their start and end apart: 3 -> 1, of which waited for: 2 -> 1; matrix products, arithmetic and copies ran while one was open for 20% -> 1% of each run, Pallas kernels for 0% -> 0%
where the time goes in v1:
time: 430 us; the launch traced here: 424 us
  matrix products  99.6 us (23%)
  local copies, waits for them, and re-layouts  91.8 us (21%)
  blocking collectives  84.8 us (20%)
  waiting for transfers between devices  75.2 us (17%)
  other arithmetic  64.4 us (15%)
  starting transfers between devices  7.08 us (2%)
    all_to_all x1, blocking collectives, body(): lax.all_to_all(leaving, ('band', 'lev'), split_axis=0, concat_axis=0, til...  84.8 us
    all_to_all x1, waiting for transfers between devices, body(): lax.all_to_all(outgoing, ('band', 'lev'), split_axis=0, concat_axis=0, ti...  75.2 us
    neg x1, other arithmetic, body(): table_cos, table_neg = lax.optimization_barrier((fine_cos, -fine_sin))  24.6 us
    dot_general x1, matrix products, body(): analysed = jnp.einsum('sjc,sjr->scr', legendre, arrived, precision=high)  19.3 us
    dot_general x1, matrix products, body(): part_neg = jnp.einsum('pyb,pbm->pym', folded, table_neg, precision=high)  18.7 us
    dot_general x1, matrix products, body(): part_cos = jnp.einsum('pyb,pbm->pym', folded, table_cos, precision=high)  18.3 us
    transpose x1, local copies, waits for them, and re-layouts, body(): arrived = jnp.transpose(arrived, (2, 0, 4, 3, 1, 5))  17.1 us
    dot_general x1, matrix products, body(): cells = jnp.einsum('pym,pbm->pyb', turned_real, table_cos, precision=high)  16.4 us
  transfers between devices with their start and end apart: 1, of which 1 were waited for; matrix products, arithmetic and copies ran while one was open for 1% of the time, Pallas kernels for 0%

profile of v1, /device:TPU:1, one launch (start us, length us, event | category | flops | bytes accessed | tf_op | source)
XLA Modules:
  0.0 423.8 jit_solution(1787707777153460565)
XLA Ops:
  0.0 0.8 select_reduce_fusion
  0.9 0.1 copy.37
  1.0 0.1 reshape.589
  1.2 0.6 multiply_convert_fusion
  1.8 0.5 iota_convert_fusion
  2.3 4.9 %add.426 = f32[3,4,24,2,1536]{4,3,2,1,0:T(2,128)S(1)} add(f32[3,4,24,2,1536]{4,3,2,1,0:T(2,128)} %param.7, f32[3,4,24,2,1536]{4,3,2,1,0:T(2,128)} %param.8) | non-fusion elementwise | flops 884736 | bytes 10616832 | tf_op jit(solution)/shard_map/add | solution.py:65
  7.2 0.6 copy.38
  7.9 3.0 reshape.590
  10.9 2.9 fusion.21
  13.7 0.9 copy-done
  14.6 1.7 subtract_bitcast_fusion
  16.3 0.6 fusion.41
  16.9 0.0 copy-done.10
  16.9 0.7 broadcast_multiply_fusion.3
  17.6 0.0 copy-done.9
  17.6 0.1 broadcast_multiply_fusion
  17.7 1.3 dynamic-slice_divide_fusion
  19.1 24.6 %fusion.1 = (f32[24,256,768]{2,1,0:T(8,128)}, f32[24,256,768]{2,1,0:T(8,128)}) fusion(f32[24]{0:T(128)S(1)} %get-tuple-element.29, f32[24]{0:T(128)S(1)} %get-tuple-element.28, f32[256,768]{1,0:T(8,128)S(1)} %broadcast_multiply_fusion), kind=kLoop, calls=%fused_computation.4 | loop fusion | flops 165150720 | bytes 38535360 | tf_op jit(solution)/shard_map/neg | solution.py:53
  43.7 0.0 copy-done.8
  43.7 0.0 copy-done.1
  43.7 0.4 maximum_bitcast_fusion
  44.1 1.1 copy.42
  45.3 0.1 broadcast_compare_fusion
  45.4 0.6 copy-done.2
  46.0 0.2 bitcast_select_fusion
  46.2 18.3 %fusion.19 = f32[24,144,768]{2,1,0:T(8,128)} fusion(f32[24,256,768]{2,1,0:T(8,128)} %get-tuple-element.7, f32[24,144,256]{2,0,1:T(8,128)S(1)} %bitcast_select_fusion), kind=kOutput, calls=%fused_computation.36 | convolution fusion | flops 4076863488 | bytes 33030144 | tf_op jit(solution)/shard_map/pyb,pbm->pym/dot_general | solution.py:71
  64.5 18.7 %fusion.17 = f32[24,144,768]{2,1,0:T(8,128)} fusion(f32[24,256,768]{2,1,0:T(8,128)} %get-tuple-element.8, f32[24,144,256]{2,0,1:T(8,128)S(1)} %bitcast_select_fusion), kind=kOutput, calls=%fused_computation.34 | convolution fusion | flops 4076863488 | bytes 33030144 | tf_op jit(solution)/shard_map/pyb,pbm->pym/dot_general | solution.py:72
  83.2 0.7 compare_select_fusion.1
  84.0 2.6 fusion.28
  86.6 8.9 %add_reduce_fusion = (f32[24,24,768]{2,1,0:T(8,128)S(1)}, f32[24,24,768]{2,1,0:T(8,128)S(1)}) fusion(f32[24,6,24,768]{3,2,1,0:T(8,128)} %bitcast.79, f32[24,6,24,768]{3,2,1,0:T(8,128)} %bitcast.78, f32[24,6,768]{2,1,0:T(8,128)S(1)} %get-tuple-element.23, f32[24,6,768]{2,1,0:T(8,128)S(1)} %get-tuple-element.24), kind=kLoop, calls=%fused_computation.16 | loop fusion | flops 20348928 | bytes 25657344 | tf_op jit(solution)/shard_map/reduce_sum | solution.py:75
  95.5 0.0 copy-start.7
  95.5 0.3 pad_maximum_fusion
  95.8 2.9 copy.45
  98.7 7.1 %all-to-all-start = ((f32[32,24,1152]{2,1,0:T(8,128)}), f32[32,24,1152]{2,1,0:T(8,128)S(1)}, u32[]{:S(2)}, u32[]{:S(2)}) async-start(f32[32,24,1152]{2,1,0:T(8,128)} %bitcast.84), calls=%async_computation | async-start | bytes 7077888 | tf_op jit(solution)/shard_map/all_to_all | solution.py:85
  105.9 1.3 gather_fusion
  107.1 0.1 reshape.598
  107.2 0.1 broadcast_in_dim.160
  107.3 0.1 mul.633
  107.4 0.7 broadcast_subtract_fusion.1
  108.1 0.7 fusion.33
  108.8 0.7 fusion.31
  109.5 75.2 %all-to-all-done = f32[32,24,1152]{2,1,0:T(8,128)S(1)} async-done(((f32[32,24,1152]{2,1,0:T(8,128)}), f32[32,24,1152]{2,1,0:T(8,128)S(1)}, u32[]{:S(2)}, u32[]{:S(2)}) %all-to-all-start) | async-done | bytes 3538976 | tf_op jit(solution)/shard_map/all_to_all | solution.py:85
  184.8 6.1 %reshape.596 = f32[16,2,12,2,24,48]{5,4,3,2,1,0:T(8,128)} reshape(f32[32,24,1152]{2,1,0:T(8,128)S(1)} %all-to-all-done) | data formatting | bytes 7077888 | tf_op jit(solution)/shard_map/reshape | solution.py:86
  190.9 17.1 %copy.46 = f32[12,16,24,2,2,48]{5,4,3,2,1,0:T(2,128)} copy(f32[12,16,24,2,2,48]{5,2,3,0,4,1:T(8,128)} %bitcast.82) | data formatting | bytes 7077888 | tf_op jit(solution)/shard_map/transpose | solution.py:87
  208.0 11.1 %reshape.597 = f32[12,384,192]{2,1,0:T(8,128)} reshape(f32[12,16,24,2,2,48]{5,4,3,2,1,0:T(2,128)} %copy.46) | data formatting | bytes 7077888 | tf_op jit(solution)/shard_map/reshape | solution.py:90
  219.1 19.3 %fusion.42 = f32[12,192,769]{2,1,0:T(8,128)S(1)} fusion(f32[12,384,192]{2,1,0:T(8,128)} %reshape.597, f32[12,384,769]{1,2,0:T(8,128)} %param.12), kind=kOutput, calls=%fused_computation.118 | convolution fusion | flops 4082171904 | bytes 24800256 | tf_op jit(solution)/shard_map/sjc,sjr->scr/dot_general | solution.py:111
  238.4 11.1 %fusion.22 = f32[12,384,192]{1,2,0:T(8,128)S(1)} fusion(f32[12,384,769]{1,2,0:T(8,128)} %param.12, f32[12,192,769]{2,1,0:T(8,128)S(1)} %fusion.42, f32[12,769]{1,0:T(8,128)S(1)} %copy-done.4, f32[192]{0:T(256)S(1)} %mul.633, s32[12,769]{1,0:T(8,128)S(1)} %copy-done.5, s32[192]{0:T(256)S(1)} %fusion.34), kind=kOutput, calls=%fused_computation.41 | convolution fusion | flops 4092802560 | bytes 24875616 | tf_op jit(solution)/shard_map/sjc,scr->sjr/dot_general | solution.py:112
  249.5 3.4 copy.49
  252.9 12.5 %reshape.599 = f32[12,16,24,2,2,48]{5,4,3,2,1,0:T(2,128)} reshape(f32[12,384,192]{2,1,0:T(8,128)} %copy.49) | data formatting | bytes 7077888 | tf_op jit(solution)/shard_map/reshape | solution.py:114
  265.4 8.5 %copy.50 = f32[16,2,12,2,24,48]{5,4,3,2,1,0:T(8,128)} copy(f32[16,2,12,2,24,48]{5,1,3,4,0,2:T(2,128)} %bitcast.83) | data formatting | bytes 7077888 | tf_op jit(solution)/shard_map/transpose | solution.py:115
  273.9 6.4 %reshape.600 = f32[32,24,1152]{2,1,0:T(8,128)S(1)} reshape(f32[16,2,12,2,24,48]{5,4,3,2,1,0:T(8,128)} %copy.50) | data formatting | bytes 7077888 | tf_op jit(solution)/shard_map/reshape | solution.py:115
  280.4 84.8 %all_to_all.10 = f32[32,24,1152]{2,1,0:T(8,128)} all-to-all(f32[32,24,1152]{2,1,0:T(8,128)S(1)} %reshape.600), channel_id=1, replica_groups=mesh['band'=16,'lev'=2] {'band','lev'}, dimensions={0} | all-to-all | bytes 7077888 | tf_op jit(solution)/shard_map/all_to_all | solution.py:118
  365.2 3.3 copy.51
  368.5 0.2 slice_bitcast_fusion.1
  368.7 9.2 %multiply_add_fusion = (f32[24,6,24,768]{3,2,1,0:T(8,128)}, f32[24,6,24,768]{3,2,1,0:T(8,128)}) fusion(f32[24,6,768]{2,1,0:T(8,128)} %get-tuple-element.20, f32[24,24,768]{2,1,0:T(8,128)S(1)} %get-tuple-element.16, f32[24,6,768]{2,1,0:T(8,128)} %get-tuple-element.19, f32[24,24,768]{2,1,0:T(8,128)S(1)} %get-tuple-element.15), kind=kLoop, calls=%fused_computation.13 | loop fusion | flops 15925248 | bytes 25657344 | tf_op jit(solution)/shard_map/add | solution.py:122
  377.9 16.4 %fusion.43 = f32[24,144,256]{2,1,0:T(8,128)} fusion(f32[24,144,768]{2,1,0:T(8,128)} %bitcast.81, f32[24,256,768]{2,1,0:T(8,128)} %get-tuple-element.7), kind=kOutput, calls=%fused_computation.119 | convolution fusion | flops 4076863488 | bytes 33030144 | tf_op jit(solution)/shard_map/pym,pbm->pyb/dot_general | solution.py:125
  394.3 15.9 %convolution_add_fusion = f32[24,144,256]{2,1,0:T(8,128)S(1)} fusion(f32[24,144,256]{2,1,0:T(8,128)} %fusion.43, f32[24,144,768]{2,1,0:T(8,128)} %bitcast.80, f32[24,256,768]{2,1,0:T(8,128)} %get-tuple-element.8), kind=kOutput, calls=%fused_computation.42 | convolution fusion | flops 4077748224 | bytes 36569088 | tf_op jit(solution)/shard_map/pym,pbm->pyb/dot_general | solution.py:126
  410.2 2.1 copy.52
  412.3 0.3 broadcast_select_fusion
  412.6 0.2 fusion.23
  412.9 0.2 subtract_bitcast_fusion.1
  413.1 0.3 maximum_bitcast_fusion.1
  413.4 4.3 %copy.59 = f32[12,24,2,6,256]{4,3,2,1,0:T(8,128)} copy(f32[12,24,2,6,256]{4,1,0,3,2:T(8,128)S(1)} %maximum_bitcast_fusion.1) | data formatting | bytes 7077888 | tf_op jit(solution)/shard_map/reshape | solution.py:133
  417.6 5.7 %reshape.613 = f32[3,4,24,2,1536]{4,3,2,1,0:T(2,128)} reshape(f32[12,24,2,6,256]{4,3,2,1,0:T(8,128)} %copy.59) | data formatting | bytes 7077888 | tf_op jit(solution)/shard_map/reshape | solution.py:133
  (28 shorter events, 0.1 us)
Async XLA Ops:
  10.9 3.8 copy-start
  10.9 5.5 %copy-start.6 = (s32[24]{0:T(128)S(1)}, s32[24]{0:T(128)}, u32[]{:S(2)}) copy-start(s32[24]{0:T(128)} %param.9) | copy-start | bytes 292
  10.9 6.1 %copy-start.10 = (f32[6]{0:T(128)S(1)}, f32[6]{0:T(128)}, u32[]{:S(2)}) copy-start(f32[6]{0:T(128)} %multiply_convert_fusion) | copy-start | bytes 76
  10.9 6.7 %copy-start.9 = (f32[256]{0:T(256)S(1)}, f32[256]{0:T(256)}, u32[]{:S(2)}) copy-start(f32[256]{0:T(256)} %iota_convert_fusion) | copy-start | bytes 3076
  16.9 26.7 %copy-start.8 = (f32[24]{0:T(128)}, f32[24]{0:T(128)S(1)}, u32[]{:S(2)}) copy-start(f32[24]{0:T(128)S(1)} %get-tuple-element.29) | copy-start | bytes 292
  19.1 24.6 %copy-start.1 = (f32[1,12,24,6,256]{4,3,2,1,0:T(8,128)S(1)}, f32[1,12,24,6,256]{4,3,2,1,0:T(8,128)}, u32[]{:S(2)}) copy-start(f32[1,12,24,6,256]{4,3,2,1,0:T(8,128)} %subtract_bitcast_fusion) | copy-start | bytes 5308420
  45.4 0.6 copy-start.2
  95.5 11.6 %copy-start.7 = (f32[3,8]{1,0:T(4,128)S(1)}, f32[3,8]{1,0:T(4,128)}, u32[]{:S(2)}) copy-start(f32[3,8]{1,0:T(4,128)} %param.13) | copy-start | bytes 292
  98.7 86.0 %all-to-all-start = ((f32[32,24,1152]{2,1,0:T(8,128)}), f32[32,24,1152]{2,1,0:T(8,128)S(1)}, u32[]{:S(2)}, u32[]{:S(2)}) async-start(f32[32,24,1152]{2,1,0:T(8,128)} %bitcast.84), calls=%async_computation | async-start | bytes 7077888 | tf_op jit(solution)/shard_map/all_to_all | solution.py:85
  219.1 19.3 %copy-start.4 = (f32[12,769]{1,0:T(8,128)S(1)}, f32[12,769]{1,0:T(8,128)}, u32[]{:S(2)}) copy-start(f32[12,769]{1,0:T(8,128)} %fusion.33) | copy-start | bytes 110740
  219.1 19.3 %copy-start.5 = (s32[12,769]{1,0:T(8,128)S(1)}, s32[12,769]{1,0:T(8,128)}, u32[]{:S(2)}) copy-start(s32[12,769]{1,0:T(8,128)} %fusion.31) | copy-start | bytes 110740
  394.3 18.0 %copy-start.3 = (pred[24,6,256]{2,0,1:T(8,128)(4,1)S(1)}, pred[24,6,256]{2,0,1:T(8,128)(4,1)}, u32[]{:S(2)}) copy-start(pred[24,6,256]{2,0,1:T(8,128)(4,1)} %copy-done.2) | copy-start | bytes 110596

commit v2 on v1

--- a/solution.py
+++ b/solution.py
@@ -84,7 +84,11 @@
     )
     arrived = lax.all_to_all(outgoing, ("band", "lev"), split_axis=0, concat_axis=0, tiled=True)
     arrived = arrived.reshape(band_count, level_groups, slot_count, 2, band_pairs, width)
-    arrived = jnp.transpose(arrived, (2, 0, 4, 3, 1, 5))
+    arrived = jnp.concatenate(
+        [arrived[:, level, :, member] for member in range(2) for level in range(level_groups)],
+        axis=3,
+    )
+    arrived = jnp.transpose(arrived, (1, 0, 2, 3))
     lat_count = band_count * band_pairs
     row_width = 2 * level_groups * width
     arrived = arrived.reshape(slot_count, lat_count, row_width)

time: 430 us -> 416 us (0.967)
  local copies, waits for them, and re-layouts: 91.8 us -> 73.2 us
  other arithmetic: 64.4 us -> 69.9 us
    transpose x1, local copies, waits for them, and re-layouts: 17.1 us -> 0.41 us  [body(): arrived = jnp.transpose(arrived, (1, 0, 2, 3))]
    reshape x1 -> x0, local copies, waits for them, and re-layouts: 11.1 us -> none  [body(): arrived = arrived.reshape(slot_count, lat_count, row_width)]
    squeeze x0 -> x1, local copies, waits for them, and re-layouts: none -> 6.97 us  [body(): arrived[:, level, :, member]]
    transpose x0 -> x1, other arithmetic: none -> 5.62 us  [body(): arrived = jnp.transpose(arrived, (1, 0, 2, 3))]
where the time goes in v2:
time: 416 us; the launch traced here: 410 us
  matrix products  99.3 us (24%)
  blocking collectives  84.8 us (20%)
  waiting for transfers between devices  75.3 us (18%)
  local copies, waits for them, and re-layouts  73.2 us (18%)
  other arithmetic  69.9 us (17%)
  starting transfers between devices  7.08 us (2%)
    all_to_all x1, blocking collectives, body(): lax.all_to_all(leaving, ('band', 'lev'), split_axis=0, concat_axis=0, til...  84.8 us
    all_to_all x1, waiting for transfers between devices, body(): lax.all_to_all(outgoing, ('band', 'lev'), split_axis=0, concat_axis=0, ti...  75.3 us
    neg x1, other arithmetic, body(): table_cos, table_neg = lax.optimization_barrier((fine_cos, -fine_sin))  24.6 us
    dot_general x1, matrix products, body(): part_neg = jnp.einsum('pyb,pbm->pym', folded, table_neg, precision=high)  18.8 us
    dot_general x1, matrix products, body(): part_cos = jnp.einsum('pyb,pbm->pym', folded, table_cos, precision=high)  18.3 us
    dot_general x1, matrix products, body(): analysed = jnp.einsum('sjc,sjr->scr', legendre, arrived, precision=high)  17.9 us
    dot_general x1, matrix products, body(): cells = jnp.einsum('pym,pbm->pyb', turned_real, table_cos, precision=high)  16.3 us
    dot_general x1, matrix products, body(): jnp.einsum('pym,pbm->pyb', turned_imag, table_neg, precision=high)  15.9 us
  transfers between devices with their start and end apart: 1, of which 1 were waited for; matrix products, arithmetic and copies ran while one was open for 1% of the time, Pallas kernels for 0%

profile of v2, /device:TPU:1, one launch (start us, length us, event | category | flops | bytes accessed | tf_op | source)
XLA Modules:
  0.0 410.4 jit_solution(12216179097753386578)
XLA Ops:
  0.0 0.8 select_reduce_fusion
  0.9 0.1 copy.42
  1.0 0.1 reshape.589
  1.2 0.5 multiply_convert_fusion
  1.7 0.5 iota_convert_fusion
  2.3 4.9 %add.426 = f32[3,4,24,2,1536]{4,3,2,1,0:T(2,128)S(1)} add(f32[3,4,24,2,1536]{4,3,2,1,0:T(2,128)} %param.7, f32[3,4,24,2,1536]{4,3,2,1,0:T(2,128)} %param.8) | non-fusion elementwise | flops 884736 | bytes 10616832 | tf_op jit(solution)/shard_map/add | solution.py:65
  7.2 0.6 copy.43
  7.8 3.0 reshape.590
  10.8 2.9 fusion.21
  13.7 0.9 copy-done
  14.6 1.7 subtract_bitcast_fusion
  16.3 0.5 fusion.41
  16.8 0.7 broadcast_multiply_fusion.3
  17.5 0.0 copy-done.9
  17.5 0.1 broadcast_multiply_fusion
  17.6 1.3 dynamic-slice_divide_fusion
  19.0 24.6 %fusion.1 = (f32[24,256,768]{2,1,0:T(8,128)}, f32[24,256,768]{2,1,0:T(8,128)}) fusion(f32[24]{0:T(128)S(1)} %get-tuple-element.33, f32[24]{0:T(128)S(1)} %get-tuple-element.32, f32[256,768]{1,0:T(8,128)S(1)} %broadcast_multiply_fusion), kind=kLoop, calls=%fused_computation.4 | loop fusion | flops 165150720 | bytes 38535360 | tf_op jit(solution)/shard_map/neg | solution.py:53
  43.6 0.0 copy-done.8
  43.6 0.0 copy-done.1
  43.6 0.4 maximum_bitcast_fusion
  44.0 1.1 copy.47
  45.2 0.1 broadcast_compare_fusion
  45.3 0.6 copy-done.2
  45.9 0.2 bitcast_select_fusion
  46.1 18.3 %fusion.19 = f32[24,144,768]{2,1,0:T(8,128)} fusion(f32[24,256,768]{2,1,0:T(8,128)} %get-tuple-element.7, f32[24,144,256]{2,0,1:T(8,128)S(1)} %bitcast_select_fusion), kind=kOutput, calls=%fused_computation.37 | convolution fusion | flops 4076863488 | bytes 33030144 | tf_op jit(solution)/shard_map/pyb,pbm->pym/dot_general | solution.py:71
  64.4 18.8 %fusion.17 = f32[24,144,768]{2,1,0:T(8,128)} fusion(f32[24,256,768]{2,1,0:T(8,128)} %get-tuple-element.8, f32[24,144,256]{2,0,1:T(8,128)S(1)} %bitcast_select_fusion), kind=kOutput, calls=%fused_computation.35 | convolution fusion | flops 4076863488 | bytes 33030144 | tf_op jit(solution)/shard_map/pyb,pbm->pym/dot_general | solution.py:72
  83.2 0.7 compare_select_fusion.1
  83.9 2.6 fusion.28
  86.5 8.9 %add_reduce_fusion = (f32[24,24,768]{2,1,0:T(8,128)S(1)}, f32[24,24,768]{2,1,0:T(8,128)S(1)}) fusion(f32[24,6,24,768]{3,2,1,0:T(8,128)} %bitcast.93, f32[24,6,24,768]{3,2,1,0:T(8,128)} %bitcast.92, f32[24,6,768]{2,1,0:T(8,128)S(1)} %get-tuple-element.27, f32[24,6,768]{2,1,0:T(8,128)S(1)} %get-tuple-element.28), kind=kLoop, calls=%fused_computation.16 | loop fusion | flops 20348928 | bytes 25657344 | tf_op jit(solution)/shard_map/reduce_sum | solution.py:75
  95.4 0.3 pad_maximum_fusion
  95.7 0.0 copy-start.7
  95.7 2.9 copy.50
  98.7 7.1 %all-to-all-start = ((f32[32,24,1152]{2,1,0:T(8,128)}), f32[32,24,1152]{2,1,0:T(8,128)S(1)}, u32[]{:S(2)}, u32[]{:S(2)}) async-start(f32[32,24,1152]{2,1,0:T(8,128)} %bitcast.100), calls=%async_computation | async-start | bytes 7077888 | tf_op jit(solution)/shard_map/all_to_all | solution.py:85
  105.8 1.2 gather_fusion
  107.0 0.1 reshape.598
  107.1 0.1 broadcast_in_dim.160
  107.2 0.1 mul.633
  107.4 0.7 broadcast_subtract_fusion.1
  108.0 0.7 fusion.33
  108.8 0.7 fusion.31
  109.5 75.3 %all-to-all-done = f32[32,24,1152]{2,1,0:T(8,128)S(1)} async-done(((f32[32,24,1152]{2,1,0:T(8,128)}), f32[32,24,1152]{2,1,0:T(8,128)S(1)}, u32[]{:S(2)}, u32[]{:S(2)}) %all-to-all-start) | async-done | bytes 3538976 | tf_op jit(solution)/shard_map/all_to_all | solution.py:85
  184.7 6.2 %reshape.596 = f32[16,2,12,2,24,48]{5,4,3,2,1,0:T(8,128)} reshape(f32[32,24,1152]{2,1,0:T(8,128)S(1)} %all-to-all-done) | data formatting | bytes 7077888 | tf_op jit(solution)/shard_map/reshape | solution.py:86
  190.9 7.0 %slice_bitcast_fusion.3 = (f32[16,12,24,48]{3,2,1,0:T(8,128)S(1)}, f32[16,12,24,48]{3,2,1,0:T(8,128)S(1)}, f32[16,12,24,48]{3,2,1,0:T(8,128)}, f32[16,12,24,48]{3,2,1,0:T(8,128)}) fusion(f32[16,2,12,2,24,48]{5,4,3,2,1,0:T(8,128)} %reshape.596), kind=kLoop, calls=%fused_computation.42 | loop fusion | bytes 7077888 | tf_op jit(solution)/shard_map/squeeze | solution.py:88
  197.9 5.6 %maximum_bitcast_fusion.1 = f32[12,16,24,192]{3,2,0,1:T(8,128)S(1)} fusion(f32[16,12,24,48]{3,2,1,0:T(8,128)} %get-tuple-element.15, f32[16,12,24,48]{3,2,1,0:T(8,128)S(1)} %get-tuple-element.14, f32[16,12,24,48]{3,2,1,0:T(8,128)} %get-tuple-element.16, f32[16,12,24,48]{3,2,1,0:T(8,128)S(1)} %get-tuple-element.13), kind=kLoop, calls=%fused_computation.25 | loop fusion | flops 2654208 | bytes 7077888 | tf_op jit(solution)/shard_map/transpose | solution.py:91
  203.5 0.4 copy.53
  204.0 17.9 %fusion.42 = f32[12,192,769]{2,1,0:T(8,128)} fusion(f32[12,384,192]{2,1,0:T(8,128)S(1)} %bitcast.97, f32[12,384,769]{1,2,0:T(8,128)S(1)} %bitcast.99), kind=kOutput, calls=%fused_computation.123 | convolution fusion | flops 4082171904 | bytes 24800256 | tf_op jit(solution)/shard_map/sjc,sjr->scr/dot_general | solution.py:115
  221.9 12.1 %fusion.22 = f32[12,384,192]{1,2,0:T(8,128)} fusion(f32[12,384,769]{1,2,0:T(8,128)S(1)} %bitcast.99, f32[12,192,769]{2,1,0:T(8,128)} %fusion.42, f32[12,769]{1,0:T(8,128)S(1)} %copy-done.4, f32[192]{0:T(256)S(1)} %mul.633, s32[12,769]{1,0:T(8,128)S(1)} %copy-done.5, s32[192]{0:T(256)S(1)} %fusion.34), kind=kOutput, calls=%fused_computation.46 | convolution fusion | flops 4092802560 | bytes 24875616 | tf_op jit(solution)/shard_map/sjc,scr->sjr/dot_general | solution.py:116
  234.0 5.5 %copy.56 = f32[12,384,192]{2,1,0:T(8,128)} copy(f32[12,384,192]{1,2,0:T(8,128)} %fusion.22) | data formatting | bytes 7077888 | tf_op jit(solution)/shard_map/sjc,scr->sjr/dot_general | solution.py:116
  239.5 12.5 %reshape.599 = f32[12,16,24,2,2,48]{5,4,3,2,1,0:T(2,128)} reshape(f32[12,384,192]{2,1,0:T(8,128)} %copy.56) | data formatting | bytes 7077888 | tf_op jit(solution)/shard_map/reshape | solution.py:118
  252.1 8.5 %copy.57 = f32[16,2,12,2,24,48]{5,4,3,2,1,0:T(8,128)} copy(f32[16,2,12,2,24,48]{5,1,3,4,0,2:T(2,128)} %bitcast.96) | data formatting | bytes 7077888 | tf_op jit(solution)/shard_map/transpose | solution.py:119
  260.6 6.4 %reshape.600 = f32[32,24,1152]{2,1,0:T(8,128)S(1)} reshape(f32[16,2,12,2,24,48]{5,4,3,2,1,0:T(8,128)} %copy.57) | data formatting | bytes 7077888 | tf_op jit(solution)/shard_map/reshape | solution.py:119
  267.0 84.8 %all_to_all.10 = f32[32,24,1152]{2,1,0:T(8,128)} all-to-all(f32[32,24,1152]{2,1,0:T(8,128)S(1)} %reshape.600), channel_id=1, replica_groups=mesh['band'=16,'lev'=2] {'band','lev'}, dimensions={0} | all-to-all | bytes 7077888 | tf_op jit(solution)/shard_map/all_to_all | solution.py:122
  351.9 3.3 copy.58
  355.2 0.2 slice_bitcast_fusion.5
  355.4 9.1 %multiply_add_fusion = (f32[24,6,24,768]{3,2,1,0:T(8,128)}, f32[24,6,24,768]{3,2,1,0:T(8,128)}) fusion(f32[24,6,768]{2,1,0:T(8,128)} %get-tuple-element.24, f32[24,24,768]{2,1,0:T(8,128)S(1)} %get-tuple-element.20, f32[24,6,768]{2,1,0:T(8,128)} %get-tuple-element.23, f32[24,24,768]{2,1,0:T(8,128)S(1)} %get-tuple-element.19), kind=kLoop, calls=%fused_computation.13 | loop fusion | flops 15925248 | bytes 25657344 | tf_op jit(solution)/shard_map/add | solution.py:126
  364.5 16.3 %fusion.43 = f32[24,144,256]{2,1,0:T(8,128)} fusion(f32[24,144,768]{2,1,0:T(8,128)} %bitcast.95, f32[24,256,768]{2,1,0:T(8,128)} %get-tuple-element.7), kind=kOutput, calls=%fused_computation.124 | convolution fusion | flops 4076863488 | bytes 33030144 | tf_op jit(solution)/shard_map/pym,pbm->pyb/dot_general | solution.py:129
  380.9 15.9 %convolution_add_fusion = f32[24,144,256]{2,1,0:T(8,128)S(1)} fusion(f32[24,144,256]{2,1,0:T(8,128)} %fusion.43, f32[24,144,768]{2,1,0:T(8,128)} %bitcast.94, f32[24,256,768]{2,1,0:T(8,128)} %get-tuple-element.8), kind=kOutput, calls=%fused_computation.47 | convolution fusion | flops 4077748224 | bytes 36569088 | tf_op jit(solution)/shard_map/pym,pbm->pyb/dot_general | solution.py:130
  396.8 2.1 copy.59
  398.9 0.3 broadcast_select_fusion
  399.2 0.2 fusion.23
  399.5 0.2 subtract_bitcast_fusion.1
  399.7 0.3 maximum_bitcast_fusion.2
  399.9 4.3 %copy.66 = f32[12,24,2,6,256]{4,3,2,1,0:T(8,128)} copy(f32[12,24,2,6,256]{4,1,0,3,2:T(8,128)S(1)} %maximum_bitcast_fusion.2) | data formatting | bytes 7077888 | tf_op jit(solution)/shard_map/reshape | solution.py:137
  404.2 5.7 %reshape.613 = f32[3,4,24,2,1536]{4,3,2,1,0:T(2,128)} reshape(f32[12,24,2,6,256]{4,3,2,1,0:T(8,128)} %copy.66) | data formatting | bytes 7077888 | tf_op jit(solution)/shard_map/reshape | solution.py:137
  (38 shorter events, 0.1 us)
Async XLA Ops:
  10.8 3.8 copy-start
  10.8 5.5 %copy-start.6 = (s32[24]{0:T(128)S(1)}, s32[24]{0:T(128)}, u32[]{:S(2)}) copy-start(s32[24]{0:T(128)} %param.9) | copy-start | bytes 292
  10.8 6.0 %copy-start.10 = (f32[6]{0:T(128)S(1)}, f32[6]{0:T(128)}, u32[]{:S(2)}) copy-start(f32[6]{0:T(128)} %multiply_convert_fusion) | copy-start | bytes 76
  10.8 6.7 %copy-start.9 = (f32[256]{0:T(256)S(1)}, f32[256]{0:T(256)}, u32[]{:S(2)}) copy-start(f32[256]{0:T(256)} %iota_convert_fusion) | copy-start | bytes 3076
  16.8 26.7 %copy-start.8 = (f32[24]{0:T(128)}, f32[24]{0:T(128)S(1)}, u32[]{:S(2)}) copy-start(f32[24]{0:T(128)S(1)} %get-tuple-element.33) | copy-start | bytes 292
  19.0 24.6 %copy-start.1 = (f32[1,12,24,6,256]{4,3,2,1,0:T(8,128)S(1)}, f32[1,12,24,6,256]{4,3,2,1,0:T(8,128)}, u32[]{:S(2)}) copy-start(f32[1,12,24,6,256]{4,3,2,1,0:T(8,128)} %subtract_bitcast_fusion) | copy-start | bytes 5308420
  45.3 0.6 copy-start.2
  95.7 11.3 %copy-start.7 = (f32[3,8]{1,0:T(4,128)S(1)}, f32[3,8]{1,0:T(4,128)}, u32[]{:S(2)}) copy-start(f32[3,8]{1,0:T(4,128)} %param.13) | copy-start | bytes 292
  98.7 86.0 %all-to-all-start = ((f32[32,24,1152]{2,1,0:T(8,128)}), f32[32,24,1152]{2,1,0:T(8,128)S(1)}, u32[]{:S(2)}, u32[]{:S(2)}) async-start(f32[32,24,1152]{2,1,0:T(8,128)} %bitcast.100), calls=%async_computation | async-start | bytes 7077888 | tf_op jit(solution)/shard_map/all_to_all | solution.py:85
  190.9 13.0 %slice-start = ((s8[14303232]{0:T(1024)(128)(4,1)}), s8[4194304]{0:T(1024)(128)(4,1)S(1)}, s32[]{:S(2)}) async-start(s8[14303232]{0:T(1024)(128)(4,1)} %bitcast.98), calls=%async_computation.2 | async-start | bytes 8388608
  190.9 13.0 %slice-start.1 = ((s8[14303232]{0:T(1024)(128)(4,1)}), s8[4194304]{0:T(1024)(128)(4,1)S(1)}, s32[]{:S(2)}) async-start(s8[14303232]{0:T(1024)(128)(4,1)} %bitcast.98), calls=%async_computation.3 | async-start | bytes 8388608
  197.9 6.1 %slice-start.2 = ((s8[14303232]{0:T(1024)(128)(4,1)}), s8[4194304]{0:T(1024)(128)(4,1)S(1)}, s32[]{:S(2)}) async-start(s8[14303232]{0:T(1024)(128)(4,1)} %bitcast.98), calls=%async_computation.4 | async-start | bytes 8388608
  197.9 6.1 %slice-start.3 = ((s8[14303232]{0:T(1024)(128)(4,1)}), s8[1720320]{0:T(1024)(128)(4,1)S(1)}, s32[]{:S(2)}) async-start(s8[14303232]{0:T(1024)(128)(4,1)} %bitcast.98), calls=%async_computation.5 | async-start | bytes 3440640
  204.0 17.9 %copy-start.4 = (f32[12,769]{1,0:T(8,128)S(1)}, f32[12,769]{1,0:T(8,128)}, u32[]{:S(2)}) copy-start(f32[12,769]{1,0:T(8,128)} %fusion.33) | copy-start | bytes 110740
  204.0 17.9 %copy-start.5 = (s32[12,769]{1,0:T(8,128)S(1)}, s32[12,769]{1,0:T(8,128)}, u32[]{:S(2)}) copy-start(s32[12,769]{1,0:T(8,128)} %fusion.31) | copy-start | bytes 110740
  380.9 18.0 %copy-start.3 = (pred[24,6,256]{2,0,1:T(8,128)(4,1)S(1)}, pred[24,6,256]{2,0,1:T(8,128)(4,1)}, u32[]{:S(2)}) copy-start(pred[24,6,256]{2,0,1:T(8,128)(4,1)} %copy-done.2) | copy-start | bytes 110596
